TPU v7x, 32 devices: a whole 2x2x4 slice. The times are simulated.
32 devices in a mesh: rep: 2 (over x), seq: 16 (over z, y, core).
Axes of the slice: x: 2, y: 2, z: 4, core: 2. Of those that a mesh axis runs over, the one named last changes fastest.
Arguments:
- projected: bfloat16 [24576, 4096], P(('rep', 'seq')), parts along dimension 0, may hold values from -6 to 6
- history_in: bfloat16 [24576, 1024], P(('rep', 'seq')), parts along dimension 0, may hold values from -6 to 6
- norm_gain: float32 [1024], replicated, may hold values from 0.1 to 1.9
- out_proj: bfloat16 [1024, 1024], replicated, may hold values from -0.1875 to 0.1875
- user_spans: int32 [16], P('rep'), parts along dimension 0, may hold values from 1 to 4, as said below
- user_tails: int32 [16], P('rep'), parts along dimension 0, may hold values from 1 to 768
- cand_emb: bfloat16 [4096, 1024], P(('rep', 'seq')), parts along dimension 0, may hold values from -6 to 6
- cand_user: int32 [4096], P(('rep', 'seq')), parts along dimension 0, may hold values from 0 to 7
- cross_down: bfloat16 [2048, 128], replicated, may hold values from -0.125 to 0.125
- cross_up: bfloat16 [128, 2048], replicated, may hold values from -0.5 to 0.5
- cross_bias: float32 [2048], replicated, may hold values from -4 to 4
- score_weight: float32 [2048], replicated, may hold values from -0.125 to 0.125
Outputs:
- history_out: bfloat16 [24576, 1024], P(('rep', 'seq')), parts along dimension 0
- scores: float32 [4096], P(('rep', 'seq')), parts along dimension 0
There are 2 independent parts, one for each index of `rep`. A program takes and returns all parts, laid end to end along the dimension named above; an argument that names none is the same for every part. Nothing has to cross between parts.
Inputs may be any that keep to these rules, and one draw needn't show every extreme that they name: `user_spans`: users own consecutive segments in order and together own all 16 segments; some user owns exactly 4.
All inputs are finite; a program needn't handle non-finite values.
Results may differ from a plain program's by a relative error of at most 0.0059.
Values may be sent and summed in bfloat16 or wider, within the bound.
A program may use at most 128 MiB of HBM per device.

v0:
```python
import functools

import jax
import jax.numpy as jnp
from jax import lax
from jax.experimental import pallas as pl
from jax.experimental.pallas import tpu as pltpu
from jax.sharding import PartitionSpec as P

HEADS = 8
MESH = pl.DeviceIdType.MESH
ONE_BACK, TWO_BACK, THREE_BACK, EVEN_OWN, OWN = range(5)


def history_kernel(
    n, row_tile, spans_ref, tails_ref, gain_ref, proj_ref, hist_ref, weight_ref, out_ref, rows_ref,
    kv, queries, gates, residual, weights, attn, final_row,
    local_sem, side_sem, send_sem, recv_sem, row_send_sem, row_recv_sem,
):
    rep, me = lax.axis_index("rep"), lax.axis_index("seq")
    core = lax.rem(me, 2)
    side = lax.rem(me // 2, 2)
    rows, width = residual.shape
    size = width // HEADS
    half_scale = 0.5 * size ** (-0.5)

    def dev(shift):
        return lax.rem(me + shift + n, n)

    partner = me + 1 - 2 * core

    def load(h, part, target, sem):
        columns = pl.ds(pl.multiple_of(part * width + h * size, size), size)
        return pltpu.make_async_copy(proj_ref.at[:, columns], target, sem)

    def loads(h):
        return (
            load(h, 2, kv.at[OWN, h, 0], local_sem.at[h, 0]),
            load(h, 3, kv.at[OWN, h, 1], local_sem.at[h, 1]),
            load(h, 1, queries.at[h], local_sem.at[h, 2]),
        )

    late = (
        pltpu.make_async_copy(proj_ref.at[:, pl.ds(0, width)], gates, side_sem.at[0]),
        pltpu.make_async_copy(hist_ref, residual, side_sem.at[1]),
        pltpu.make_async_copy(weight_ref, weights, side_sem.at[2]),
    )

    @pl.loop(0, HEADS)
    def _(h):
        for copy in loads(h):
            copy.start()

    for copy in late:
        copy.start()

    barrier = pltpu.get_barrier_semaphore()

    @pl.loop(1, n)
    def _(shift):
        pl.semaphore_signal(
            barrier, inc=1, device_id=(rep, dev(shift)), device_id_type=MESH
        )

    def scan_user(user, found):
        start, first, last, tail = found
        end = start + spans_ref[user]
        mine = (start <= me) & (me < end)
        return (
            end,
            jnp.where(mine, start, first),
            jnp.where(mine, end - 1, last),
            jnp.where(mine, tails_ref[user], tail),
        )

    zero = jnp.int32(0)
    _, first, last, tail = lax.fori_loop(
        0, spans_ref.shape[0], scan_user, (zero, zero, zero, zero)
    )
    valid = jnp.where(me == last, tail, rows)

    pl.semaphore_wait(barrier, n - 1)

    def push(h, source, slot, target, use):
        return pltpu.make_async_remote_copy(
            src_ref=kv.at[source, h],
            dst_ref=kv.at[slot, h],
            send_sem=send_sem.at[use, h],
            recv_sem=recv_sem.at[slot, h],
            device_id=(rep, target),
            device_id_type=MESH,
        )

    def arrived(h, slot):
        push(h, slot, slot, partner, 0).wait_recv()

    def sent(h, use):
        push(h, OWN, OWN, partner, use).wait_send()

    @pl.loop(0, HEADS)
    def _(h):
        for copy in loads(h):
            copy.wait()

        @pl.when(core == 0)
        def _():
            push(h, OWN, TWO_BACK, dev(2), 0).start()
            push(h, OWN, EVEN_OWN, partner, 2).start()

        @pl.when(core == 1)
        def _():
            push(h, OWN, THREE_BACK, dev(4), 1).start()

            @pl.when(side == 0)
            def _():
                push(h, OWN, ONE_BACK, dev(2), 0).start()

    def weigh(q, k):
        half = half_scale * lax.dot_general(
            q, k, (((1,), (1,)), ((), ())), preferred_element_type=jnp.float32
        )
        return half + half * jnp.tanh(half)

    tiles = rows // row_tile
    causal = lax.broadcasted_iota(jnp.int32, (row_tile, row_tile), 1) <= (
        lax.broadcasted_iota(jnp.int32, (row_tile, row_tile), 0)
    )

    def head_columns(h):
        return pl.ds(pl.multiple_of(h * size, size), size)

    @pl.loop(0, HEADS)
    def _(h):
        for tile in range(tiles):
            low, high = tile * row_tile, (tile + 1) * row_tile
            q = queries[h, low:high]
            edge = jnp.where(causal, weigh(q, kv[OWN, h, 0, low:high]), 0.0).astype(jnp.bfloat16)
            total = jnp.dot(edge, kv[OWN, h, 1, low:high], preferred_element_type=jnp.float32)
            if tile:
                full = weigh(q, kv[OWN, h, 0, :low]).astype(jnp.bfloat16)
                total += jnp.dot(full, kv[OWN, h, 1, :low], preferred_element_type=jnp.float32)
            attn[low:high, head_columns(h)] = total

    def absorb(h, blocks):
        for tile in range(tiles):
            low, high = tile * row_tile, (tile + 1) * row_tile
            q = queries[h, low:high]
            total = attn[low:high, head_columns(h)]
            for slot, back in blocks:
                w = weigh(q, kv[slot, h, 0]).astype(jnp.bfloat16)
                part = jnp.dot(w, kv[slot, h, 1], preferred_element_type=jnp.float32)
                total += jnp.where(me - back >= first, part, 0.0)
            attn[low:high, head_columns(h)] = total

    @pl.loop(0, HEADS + 1)
    def _(step):
        @pl.when(step < HEADS)
        def _():
            h = step

            @pl.when(core == 0)
            def _():
                arrived(h, TWO_BACK)
                push(h, TWO_BACK, TWO_BACK, partner, 3).start()

            @pl.when(core == 1)
            def _():
                arrived(h, EVEN_OWN)
                absorb(h, ((EVEN_OWN, 1),))
                arrived(h, THREE_BACK)

                @pl.when(side == 1)
                def _():
                    push(h, THREE_BACK, ONE_BACK, dev(-2), 0).start()

                push(h, THREE_BACK, THREE_BACK, partner, 2).start()

                @pl.when(side == 1)
                def _():
                    arrived(h, ONE_BACK)
                    push(h, ONE_BACK, ONE_BACK, partner, 3).start()

        @pl.when(step >= 1)
        def _():
            h = step - 1

            @pl.when(core == 0)
            def _():
                arrived(h, ONE_BACK)
                arrived(h, THREE_BACK)
                absorb(h, ((ONE_BACK, 1), (TWO_BACK, 2), (THREE_BACK, 3)))

            @pl.when(core == 1)
            def _():
                @pl.when(side == 0)
                def _():
                    arrived(h, ONE_BACK)
                    push(h, ONE_BACK, ONE_BACK, partner, 3).start()

                arrived(h, TWO_BACK)
                absorb(h, ((ONE_BACK, 2), (TWO_BACK, 3)))

    for copy in late:
        copy.wait()
    gain = gain_ref[...]

    def finish(x, gate, rest):
        centered = x - jnp.mean(x, axis=1, keepdims=True)
        var = jnp.mean(centered * centered, axis=1, keepdims=True)
        normed = centered * lax.rsqrt(var + 1e-06) * gain
        gated = (normed * gate.astype(jnp.float32)).astype(jnp.bfloat16)
        out = jnp.dot(gated, weights[...], preferred_element_type=jnp.float32)
        return (out + rest.astype(jnp.float32)).astype(jnp.bfloat16)

    final = jnp.clip(valid - 1, 0, rows - 1)
    at_last = lax.broadcasted_iota(jnp.int32, (16, rows), 1) == final
    pick = jnp.where(at_last, 1.0, 0.0).astype(jnp.bfloat16)
    picked = finish(
        jnp.broadcast_to(attn[pl.ds(final, 1), :], (16, width)),
        jnp.dot(pick, gates[...], preferred_element_type=jnp.float32),
        jnp.dot(pick, residual[...], preferred_element_type=jnp.float32),
    ).astype(jnp.float32)[0:1]
    final_row[...] = picked
    rows_ref[me] = picked

    def row_to(shift):
        return pltpu.make_async_remote_copy(
            src_ref=final_row,
            dst_ref=rows_ref.at[me],
            send_sem=row_send_sem.at[shift],
            recv_sem=row_recv_sem.at[shift],
            device_id=(rep, dev(shift)),
            device_id_type=MESH,
        )

    for tile in range(tiles):
        low, high = tile * row_tile, (tile + 1) * row_tile
        ids = low + lax.broadcasted_iota(jnp.int32, (row_tile, 1), 0)
        x = jnp.where(ids < valid, attn[low:high], 0.0)
        out_ref[low:high] = finish(x, gates[low:high], residual[low:high])
        if tile == 0:

            @pl.loop(1, n)
            def _(shift):
                row_to(shift).start()

    @pl.loop(1, n)
    def _(shift):
        row_to(shift).wait_send()
        row_to(shift).wait_recv()

    @pl.loop(0, HEADS)
    def _(h):
        sent(h, 2)
        sent(h, 3)
        sent(h, 0)

        @pl.when(core == 1)
        def _():
            sent(h, 1)


def history_layer(n, spans, tails, gain, projected, history_in, out_proj):
    rows, width = history_in.shape
    size = width // HEADS
    row_tile = next(t for t in (384, 256, 128, 64, 32, 16, rows) if rows % t == 0)
    smem = pl.BlockSpec(memory_space=pltpu.SMEM)
    anywhere = pl.BlockSpec(memory_space=pl.ANY)
    vmem = pl.BlockSpec(memory_space=pltpu.VMEM)
    return pl.pallas_call(
        functools.partial(history_kernel, n, row_tile),
        out_shape=(
            jax.ShapeDtypeStruct((rows, width), jnp.bfloat16),
            jax.ShapeDtypeStruct((n, 1, width), jnp.float32),
        ),
        in_specs=[smem, smem, vmem, anywhere, anywhere, anywhere],
        out_specs=(vmem, vmem),
        scratch_shapes=[
            pltpu.VMEM((5, HEADS, 2, rows, size), jnp.bfloat16),
            pltpu.VMEM((HEADS, rows, size), jnp.bfloat16),
            pltpu.VMEM((rows, width), jnp.bfloat16),
            pltpu.VMEM((rows, width), jnp.bfloat16),
            pltpu.VMEM((width, width), jnp.bfloat16),
            pltpu.VMEM((rows, width), jnp.float32),
            pltpu.VMEM((1, width), jnp.float32),
            pltpu.SemaphoreType.DMA((HEADS, 3)),
            pltpu.SemaphoreType.DMA((3,)),
            pltpu.SemaphoreType.DMA((4, HEADS)),
            pltpu.SemaphoreType.DMA((5, HEADS)),
            pltpu.SemaphoreType.DMA((n,)),
            pltpu.SemaphoreType.DMA((n,)),
        ],
        compiler_params=pltpu.CompilerParams(
            collective_id=0, has_side_effects=True, vmem_limit_bytes=60 * 1024 * 1024
        ),
        name="history_layer",
    )(spans, tails, gain, projected, history_in, out_proj)


def body(
    projected,
    history_in,
    norm_gain,
    out_proj,
    user_spans,
    user_tails,
    cand_emb,
    cand_user,
    cross_down,
    cross_up,
    cross_bias,
    score_weight,
):
    model_width = history_in.shape[1]
    devices = lax.axis_size("seq")
    history_out, user_rows = history_layer(
        devices, user_spans, user_tails, norm_gain[None, :], projected, history_in, out_proj
    )
    user_rows = user_rows.reshape(devices, model_width).astype(jnp.bfloat16)
    device_ids = jnp.arange(devices, dtype=jnp.int32)
    user_count = user_spans.shape[0]
    users = jnp.arange(user_count, dtype=jnp.int32)
    last_dev = jnp.sum(jnp.where(users[None, :] <= users[:, None], user_spans[None, :], 0), axis=1) - 1
    user_match = cand_user[:, None] == jnp.arange(user_count, dtype=jnp.int32)[None, :]
    cand_dev = jnp.sum(jnp.where(user_match, last_dev[None, :], 0), axis=1)
    selector = (cand_dev[:, None] == device_ids[None, :]).astype(jnp.bfloat16)
    user_part = jnp.dot(selector, user_rows, preferred_element_type=jnp.float32).astype(
        jnp.bfloat16
    )
    crossed_in = jnp.concatenate([user_part, cand_emb], axis=1)
    low_rank = jnp.dot(crossed_in, cross_down, preferred_element_type=jnp.float32).astype(
        jnp.bfloat16
    )
    up_part = jnp.dot(low_rank, cross_up, preferred_element_type=jnp.float32)
    input_float = crossed_in.astype(jnp.float32)
    crossed = input_float * (up_part + cross_bias) + input_float
    scores = jnp.sum(crossed * score_weight, axis=1)
    return (history_out, scores)


def solution(mesh):
    in_specs = (
        P(("rep", "seq"), None),
        P(("rep", "seq"), None),
        P(),
        P(),
        P("rep"),
        P("rep"),
        P(("rep", "seq"), None),
        P(("rep", "seq")),
        P(),
        P(),
        P(),
        P(),
    )
    out_specs = (P(("rep", "seq"), None), P(("rep", "seq")))
    return jax.shard_map(body, mesh=mesh, in_specs=in_specs, out_specs=out_specs, check_vma=False)
```

profile of v0, /device:TPU:0, one launch (start us, length us, event | category | flops | bytes accessed | tf_op | source)
XLA Modules:
  0.0 96.8 jit_solution(1076013658839860968)
XLA Ops:
  0.6 0.0 copy-start
  0.6 0.0 copy-start.2
  0.7 0.0 copy-start.7
  0.7 0.0 copy-start.3
  0.7 0.0 copy-start.4
  0.7 0.0 copy-start.5
  0.7 0.0 copy-start.6
  0.7 92.1 %history_layer.1 = (bf16[768,1024]{1,0:T(8,128)(2,1)}, f32[16,1,1024]{2,1,0:T(1,128)}) custom-call(s32[8]{0:T(128)} %spans_ref.1, s32[8]{0:T(128)} %tails_ref.1, f32[1,1024]{1,0:T(1,128)} %bitcast.6, bf16[768,4096]{1,0:T(8,128)(2,1)} %proj_ref.1, bf16[768,1024]{1,0:T(8,128)(2,1)} %hist_ref.1, bf16[1024,1024]{1,0:T(8,128)(2,1)} %weight_ref.1), custom_call_target="tpu_custom_call" | custom-call | tf_op jit(solution)/shard_map/history_layer/pallas_call | solution.py:270
  92.8 0.9 convert_element_type.16
  93.7 0.0 copy-done.2
  93.7 0.1 select_reduce_fusion.1
  93.8 0.0 copy-done.7
  93.8 0.1 select_reduce_fusion
  93.9 0.3 convolution_convert_fusion
  94.2 0.0 copy-done
  94.2 0.0 copy-done.3
  94.2 0.0 copy-done.4
  94.2 0.0 copy-done.5
  94.2 0.0 copy-done.6
  94.2 0.0 copy-start.1
  94.2 1.2 %fusion.3 = f32[128]{0:T(128)} fusion(bf16[128,2048]{1,0:T(8,128)(2,1)S(1)} %copy-done, bf16[2048,128]{1,0:T(8,128)(2,1)S(1)} %copy-done.3, bf16[128,1024]{1,0:T(8,128)(2,1)S(1)} %copy-done.4, bf16[128,1024]{1,0:T(8,128)(2,1)S(1)} %convolution_convert_fusion, f32[2048]{0:T(1024)S(1)} %copy-done.5, f32[2048]{0:T(1024)S(1)} %copy-done.6), kind=kOutput, calls=%fused_computation.4 | convolution fusion | flops 137641856 | bytes 1589760 | tf_op jit(solution)/shard_map/dot_general | solution.py:334
  95.4 0.2 copy-done.1
  95.6 1.1 %copy.20 = bf16[768,1024]{1,0:T(8,128)(2,1)} copy(bf16[768,1024]{1,0:T(8,128)(2,1)S(1)} %copy-done.1) | data formatting | bytes 3145728
  (1 shorter events, 0.0 us)
Async XLA Ops:
  0.6 93.5 %copy-start = (bf16[128,2048]{1,0:T(8,128)(2,1)S(1)}, bf16[128,2048]{1,0:T(8,128)(2,1)}, u32[]{:S(2)}) copy-start(bf16[128,2048]{1,0:T(8,128)(2,1)} %param.21) | copy-start | bytes 1572868
  0.6 93.0 %copy-start.2 = (s32[8]{0:T(128)S(1)}, s32[8]{0:T(128)}, u32[]{:S(2)}) copy-start(s32[8]{0:T(128)} %spans_ref.1) | copy-start | bytes 100
  0.7 93.2 %copy-start.7 = (s32[128]{0:T(128)S(1)}, s32[128]{0:T(128)}, u32[]{:S(2)}) copy-start(s32[128]{0:T(128)} %param.19) | copy-start | bytes 1540
  0.7 93.5 %copy-start.3 = (bf16[2048,128]{1,0:T(8,128)(2,1)S(1)}, bf16[2048,128]{1,0:T(8,128)(2,1)}, u32[]{:S(2)}) copy-start(bf16[2048,128]{1,0:T(8,128)(2,1)} %param.20) | copy-start | bytes 1572868
  0.7 93.5 %copy-start.4 = (bf16[128,1024]{1,0:T(8,128)(2,1)S(1)}, bf16[128,1024]{1,0:T(8,128)(2,1)}, u32[]{:S(2)}) copy-start(bf16[128,1024]{1,0:T(8,128)(2,1)} %param.18) | copy-start | bytes 786436
  0.7 93.5 %copy-start.5 = (f32[2048]{0:T(1024)S(1)}, f32[2048]{0:T(1024)}, u32[]{:S(2)}) copy-start(f32[2048]{0:T(1024)} %param.23) | copy-start | bytes 24580
  0.7 93.5 %copy-start.6 = (f32[2048]{0:T(1024)S(1)}, f32[2048]{0:T(1024)}, u32[]{:S(2)}) copy-start(f32[2048]{0:T(1024)} %param.22) | copy-start | bytes 24580
  94.2 1.4 %copy-start.1 = (bf16[768,1024]{1,0:T(8,128)(2,1)S(1)}, bf16[768,1024]{1,0:T(8,128)(2,1)}, u32[]{:S(2)}) copy-start(bf16[768,1024]{1,0:T(8,128)(2,1)} %get-tuple-element.8) | copy-start | bytes 4718596
where the time goes:
time: 97 us; the launch traced here: 96.8 us
  Pallas kernels  92.1 us (95%)
  matrix products  1.47 us (2%)
  local copies, waits for them, and re-layouts  1.37 us (1%)
  other arithmetic  1.09 us (1%)
    pallas_call x1, Pallas kernels, history_layer(): pl.pallas_call(functools.partial(history_kernel, n, row_tile), out_shape=...  92.1 us

commit v1 on v0

v1 whole, which is shorter than its diff:
```python
import functools

import jax
import jax.numpy as jnp
from jax import lax
from jax.experimental import pallas as pl
from jax.experimental.pallas import tpu as pltpu
from jax.sharding import PartitionSpec as P

HEADS = 8
LAG = 3
MESH = pl.DeviceIdType.MESH
OWN, PAIR = range(2)


def history_kernel(
    n, row_tile, spans_ref, tails_ref, gain_ref, proj_ref, hist_ref, weight_ref, out_ref, rows_ref,
    kv, queries, gates, residual, weights, attn, final_row, in1, in2, in3, in4, out1, out2,
    load_sem, query_sem, fill_sem, side_sem, pair_send, pair_recv, near_send, far_send, part_send, relay_send,
    recv1, recv2, recv3, recv4, row_send_sem, row_recv_sem,
):
    rep, me = lax.axis_index("rep"), lax.axis_index("seq")
    core = lax.rem(me, 2)
    side = lax.rem(me // 2, 2)
    rows, width = residual.shape
    size = width // HEADS
    half_scale = 0.5 * size ** (-0.5)
    tiles = rows // row_tile
    steps = HEADS * tiles
    partner = me + 1 - 2 * core
    even, odd = core == 0, core == 1
    slot_a, slot_b = odd & (side == 0), odd & (side == 1)

    def dev(shift):
        return lax.rem(me + shift + n, n)

    def columns(part, h):
        return pl.ds(pl.multiple_of(part * width + h * size, size), size)

    def load(h, part, target, sem):
        return pltpu.make_async_copy(proj_ref.at[:, columns(part, h)], target, sem)

    def load_queries(h, tile, target, sem):
        block = proj_ref.at[pl.ds(tile * row_tile, row_tile), columns(1, h)]
        return pltpu.make_async_copy(block, target, sem)

    def loads(h):
        return (
            load(h, 2, kv.at[OWN, h, 0], load_sem.at[h, 0]),
            load(h, 3, kv.at[OWN, h, 1], load_sem.at[h, 1]),
            *(
                load_queries(h, tile, queries.at[h * tiles + tile], query_sem.at[h * tiles + tile])
                for tile in range(tiles)
            ),
        )

    late = (
        pltpu.make_async_copy(proj_ref.at[:, pl.ds(0, width)], gates, side_sem.at[0]),
        pltpu.make_async_copy(hist_ref, residual, side_sem.at[1]),
        pltpu.make_async_copy(weight_ref, weights, side_sem.at[2]),
    )
    fills = [load_queries(s // tiles, s % tiles, out1.at[s], fill_sem.at[s]) for s in range(LAG)]
    fill_here = slot_b | (slot_a & (me + 4 >= n))

    @pl.when(fill_here)
    def _():
        for copy in fills:
            copy.start()

    @pl.loop(0, HEADS)
    def _(h):
        for copy in loads(h):
            copy.start()

    for copy in late:
        copy.start()

    barrier = pltpu.get_barrier_semaphore()

    @pl.loop(1, n)
    def _(shift):
        pl.semaphore_signal(
            barrier, inc=1, device_id=(rep, dev(shift)), device_id_type=MESH
        )

    seen = (me, me + 2, me + 4, 4 * (me // 4) + 5)

    def scan_user(user, found):
        start, last, tail, firsts = found
        end = start + spans_ref[user]
        mine = (start <= me) & (me < end)
        return (
            end,
            jnp.where(mine, end - 1, last),
            jnp.where(mine, tails_ref[user], tail),
            tuple(
                jnp.where((start <= s) & (s < end), start, first) for s, first in zip(seen, firsts)
            ),
        )

    zero = jnp.int32(0)
    _, last, tail, firsts = lax.fori_loop(
        0, spans_ref.shape[0], scan_user, (zero, zero, zero, (jnp.int32(2 * n),) * len(seen))
    )
    valid = jnp.where(me == last, tail, rows)
    first_me, first_near, first_far, first_slot = firsts
    swapped = first_slot <= 4 * (me // 4) + 3

    pl.semaphore_wait(barrier, n - 1)

    def remote(source, target, send_sem, recv_sem, device):
        return pltpu.make_async_remote_copy(
            src_ref=source,
            dst_ref=target,
            send_sem=send_sem,
            recv_sem=recv_sem,
            device_id=(rep, device),
            device_id_type=MESH,
        )

    def pair(h):
        return remote(kv.at[OWN, h], kv.at[PAIR, h], pair_send.at[h], pair_recv.at[h], partner)

    def near(s):
        return remote(queries.at[s], in1.at[s], near_send.at[s], recv1.at[s], dev(-2))

    def far(s):
        return remote(queries.at[s], in2.at[s], far_send.at[s], recv2.at[s], dev(-4))

    def far_first(s):
        return remote(queries.at[s], out1.at[s], far_send.at[s], recv2.at[s], dev(-4))

    def near_sum(s):
        return remote(out1.at[s], in3.at[s], part_send.at[s], recv3.at[s], dev(2))

    def far_sum(s):
        return remote(out2.at[s], in4.at[s], relay_send.at[s], recv4.at[s], dev(4))

    def slot(t):
        other = me + 2 - 4 * side
        return remote(out1.at[t], in1.at[t], part_send.at[t], recv1.at[t], other)

    def relay(t):
        return remote(in1.at[t], in3.at[t], relay_send.at[t], recv3.at[t], dev(4))

    @pl.loop(0, HEADS)
    def _(h):
        for copy in loads(h):
            copy.wait()
        pair(h).start()
        for tile in range(tiles):
            s = h * tiles + tile

            @pl.when(even & (me >= 2))
            def _():
                near(s).start()

            @pl.when(even & (me >= 4))
            def _():
                far(s).start()

            @pl.when(slot_a & (me >= 4))
            def _():
                @pl.when(s < LAG)
                def _():
                    far_first(s).start()

                @pl.when(s >= LAG)
                def _():
                    far(s).start()

    def weigh(q, k):
        half = half_scale * lax.dot_general(
            q, k, (((1,), (1,)), ((), ())), preferred_element_type=jnp.float32
        )
        return half + half * jnp.tanh(half)

    causal = lax.broadcasted_iota(jnp.int32, (row_tile, row_tile), 1) <= (
        lax.broadcasted_iota(jnp.int32, (row_tile, row_tile), 0)
    )

    def head_columns(h):
        return pl.ds(pl.multiple_of(h * size, size), size)

    def over(q, which, h, wanted):
        w = weigh(q, kv[which, h, 0]).astype(jnp.bfloat16)
        part = jnp.dot(w, kv[which, h, 1], preferred_element_type=jnp.float32)
        return jnp.where(wanted, part, 0.0)

    def own(h, tile):
        low, high = tile * row_tile, (tile + 1) * row_tile
        q = queries[h * tiles + tile]
        edge = jnp.where(causal, weigh(q, kv[OWN, h, 0, low:high]), 0.0).astype(jnp.bfloat16)
        total = jnp.dot(edge, kv[OWN, h, 1, low:high], preferred_element_type=jnp.float32)
        if tile:
            full = weigh(q, kv[OWN, h, 0, :low]).astype(jnp.bfloat16)
            total += jnp.dot(full, kv[OWN, h, 1, :low], preferred_element_type=jnp.float32)
        return total

    def add(h, tile, part):
        low, high = tile * row_tile, (tile + 1) * row_tile
        attn[low:high, head_columns(h)] += part.astype(jnp.float32)

    @pl.when(even)
    def _():
        @pl.loop(0, HEADS)
        def _(h):
            for tile in range(tiles):
                s = h * tiles + tile
                attn[tile * row_tile:(tile + 1) * row_tile, head_columns(h)] = own(h, tile)

                @pl.when((s >= 1) & (me + 2 < n))
                def _():
                    near_sum(s - 1).start()

                @pl.when((s >= 1) & (me + 4 < n))
                def _():
                    far_sum(s - 1).start()

                if tile == 0:
                    pair(h).wait_recv()

                @pl.when(me + 2 < n)
                def _():
                    near(s).wait_recv()
                    q = in1[s]
                    total = over(q, OWN, h, first_near <= me)
                    total += over(q, PAIR, h, first_near <= me + 1)
                    out1[s] = total.astype(jnp.bfloat16)

                @pl.when(me + 4 < n)
                def _():
                    far(s).wait_recv()
                    out2[s] = over(in2[s], PAIR, h, first_far <= me + 1).astype(jnp.bfloat16)

        @pl.when(me + 2 < n)
        def _():
            near_sum(steps - 1).start()

        @pl.when(me + 4 < n)
        def _():
            far_sum(steps - 1).start()

        @pl.when(me >= 4)
        def _():
            @pl.loop(0, HEADS)
            def _(h):
                for tile in range(tiles):
                    far_sum(h * tiles + tile).wait_recv()
                    add(h, tile, in4[h * tiles + tile])

        @pl.when(me >= 2)
        def _():
            @pl.loop(0, HEADS)
            def _(h):
                for tile in range(tiles):
                    near_sum(h * tiles + tile).wait_recv()
                    add(h, tile, in3[h * tiles + tile])

    @pl.when(odd)
    def _():
        @pl.when(fill_here)
        def _():
            for copy in fills:
                copy.wait()

        @pl.when(slot_a & (me + 4 < n))
        def _():
            for s in range(LAG):
                far_first(s).wait_recv()

        for t in range(LAG):
            slot(t).start()

        def pass_on(t):
            slot(t).wait_recv()

            @pl.when((side == 0) & (me + 4 < n))
            def _():
                relay(t).start()

        @pl.loop(0, HEADS)
        def _(h):
            for tile in range(tiles):
                t = h * tiles + tile
                if tile == 0:
                    pair(h).wait_recv()
                attn[tile * row_tile:(tile + 1) * row_tile, head_columns(h)] = own(h, tile) + over(
                    queries[t], PAIR, h, first_me <= me - 1
                )

                @pl.when(t >= 1)
                def _():
                    slot(t + LAG - 1).start()

                pass_on(t)
                q = in1[t]
                total = over(q, OWN, h, first_near <= me)
                total += over(q, PAIR, h, first_near <= me - 1)
                out1[t + LAG] = total.astype(jnp.bfloat16)

                @pl.when((t + LAG < steps) & (side == 1))
                def _():
                    out1[t + LAG] = jnp.where(swapped, out1[t + LAG], queries[t + LAG])

                @pl.when((t + LAG < steps) & (side == 0) & (me + 4 < n))
                def _():
                    far(t + LAG).wait_recv()
                    out1[t + LAG] = jnp.where(swapped, in2[t + LAG], out1[t + LAG])

        slot(steps + LAG - 1).start()

        @pl.loop(steps, steps + LAG)
        def _(t):
            pass_on(t)

        mine = first_me <= me - 2

        @pl.when(side == 1)
        def _():
            @pl.loop(0, HEADS)
            def _(h):
                for tile in range(tiles):
                    add(h, tile, jnp.where(mine, in1[h * tiles + tile + LAG], 0.0))

        @pl.when((side == 0) & (me >= 4))
        def _():
            for t in range(LAG):
                relay(t).wait_recv()

            @pl.loop(0, HEADS)
            def _(h):
                for tile in range(tiles):
                    t = h * tiles + tile + LAG
                    relay(t).wait_recv()
                    add(h, tile, jnp.where(mine, in3[t], 0.0))

    for copy in late:
        copy.wait()
    gain = gain_ref[...]

    def finish(x, gate, rest):
        centered = x - jnp.mean(x, axis=1, keepdims=True)
        var = jnp.mean(centered * centered, axis=1, keepdims=True)
        normed = centered * lax.rsqrt(var + 1e-06) * gain
        gated = (normed * gate.astype(jnp.float32)).astype(jnp.bfloat16)
        out = jnp.dot(gated, weights[...], preferred_element_type=jnp.float32)
        return (out + rest.astype(jnp.float32)).astype(jnp.bfloat16)

    final = jnp.clip(valid - 1, 0, rows - 1)
    at_last = lax.broadcasted_iota(jnp.int32, (16, rows), 1) == final
    pick = jnp.where(at_last, 1.0, 0.0).astype(jnp.bfloat16)
    picked = finish(
        jnp.broadcast_to(attn[pl.ds(final, 1), :], (16, width)),
        jnp.dot(pick, gates[...], preferred_element_type=jnp.float32),
        jnp.dot(pick, residual[...], preferred_element_type=jnp.float32),
    ).astype(jnp.float32)[0:1]
    final_row[...] = picked
    rows_ref[me] = picked

    def row_to(shift):
        return pltpu.make_async_remote_copy(
            src_ref=final_row,
            dst_ref=rows_ref.at[me],
            send_sem=row_send_sem.at[shift],
            recv_sem=row_recv_sem.at[shift],
            device_id=(rep, dev(shift)),
            device_id_type=MESH,
        )

    for tile in range(tiles):
        low, high = tile * row_tile, (tile + 1) * row_tile
        ids = low + lax.broadcasted_iota(jnp.int32, (row_tile, 1), 0)
        x = jnp.where(ids < valid, attn[low:high], 0.0)
        out_ref[low:high] = finish(x, gates[low:high], residual[low:high])
        if tile == 0:

            @pl.loop(1, n)
            def _(shift):
                row_to(shift).start()

    @pl.loop(1, n)
    def _(shift):
        row_to(shift).wait_send()
        row_to(shift).wait_recv()

    @pl.loop(0, HEADS)
    def _(h):
        pair(h).wait_send()

    @pl.loop(0, steps)
    def _(s):
        @pl.when(even & (me >= 2))
        def _():
            near(s).wait_send()

        @pl.when((even | slot_a) & (me >= 4))
        def _():
            far(s).wait_send()

        @pl.when(even & (me + 2 < n))
        def _():
            near_sum(s).wait_send()

        @pl.when(even & (me + 4 < n))
        def _():
            far_sum(s).wait_send()

    @pl.when(odd)
    def _():
        @pl.loop(0, steps + LAG)
        def _(t):
            slot(t).wait_send()

            @pl.when((side == 0) & (me + 4 < n))
            def _():
                relay(t).wait_send()


def history_layer(n, spans, tails, gain, projected, history_in, out_proj):
    rows, width = history_in.shape
    size = width // HEADS
    row_tile = next(t for t in (384, 256, 128, 64, 32, 16, rows) if rows % t == 0)
    steps = HEADS * (rows // row_tile)
    slots = steps + LAG
    smem = pl.BlockSpec(memory_space=pltpu.SMEM)
    anywhere = pl.BlockSpec(memory_space=pl.ANY)
    vmem = pl.BlockSpec(memory_space=pltpu.VMEM)
    blocks = lambda count: pltpu.VMEM((count, row_tile, size), jnp.bfloat16)
    dma = lambda *shape: pltpu.SemaphoreType.DMA(shape)
    return pl.pallas_call(
        functools.partial(history_kernel, n, row_tile),
        out_shape=(
            jax.ShapeDtypeStruct((rows, width), jnp.bfloat16),
            jax.ShapeDtypeStruct((n, 1, width), jnp.float32),
        ),
        in_specs=[smem, smem, vmem, anywhere, anywhere, anywhere],
        out_specs=(vmem, vmem),
        scratch_shapes=[
            pltpu.VMEM((2, HEADS, 2, rows, size), jnp.bfloat16),
            blocks(steps),
            pltpu.VMEM((rows, width), jnp.bfloat16),
            pltpu.VMEM((rows, width), jnp.bfloat16),
            pltpu.VMEM((width, width), jnp.bfloat16),
            pltpu.VMEM((rows, width), jnp.float32),
            pltpu.VMEM((1, width), jnp.float32),
            blocks(slots),
            blocks(steps),
            blocks(slots),
            blocks(steps),
            blocks(slots),
            blocks(steps),
            dma(HEADS, 2),
            dma(steps),
            dma(LAG),
            dma(3),
            dma(HEADS),
            dma(HEADS),
            dma(steps),
            dma(steps),
            dma(slots),
            dma(slots),
            dma(slots),
            dma(steps),
            dma(slots),
            dma(steps),
            dma(n),
            dma(n),
        ],
        compiler_params=pltpu.CompilerParams(
            collective_id=0, has_side_effects=True, vmem_limit_bytes=60 * 1024 * 1024
        ),
        name="history_layer",
    )(spans, tails, gain, projected, history_in, out_proj)


def body(
    projected,
    history_in,
    norm_gain,
    out_proj,
    user_spans,
    user_tails,
    cand_emb,
    cand_user,
    cross_down,
    cross_up,
    cross_bias,
    score_weight,
):
    model_width = history_in.shape[1]
    devices = lax.axis_size("seq")
    history_out, user_rows = history_layer(
        devices, user_spans, user_tails, norm_gain[None, :], projected, history_in, out_proj
    )
    user_rows = user_rows.reshape(devices, model_width).astype(jnp.bfloat16)
    device_ids = jnp.arange(devices, dtype=jnp.int32)
    user_count = user_spans.shape[0]
    users = jnp.arange(user_count, dtype=jnp.int32)
    last_dev = jnp.sum(jnp.where(users[None, :] <= users[:, None], user_spans[None, :], 0), axis=1) - 1
    user_match = cand_user[:, None] == jnp.arange(user_count, dtype=jnp.int32)[None, :]
    cand_dev = jnp.sum(jnp.where(user_match, last_dev[None, :], 0), axis=1)
    selector = (cand_dev[:, None] == device_ids[None, :]).astype(jnp.bfloat16)
    user_part = jnp.dot(selector, user_rows, preferred_element_type=jnp.float32).astype(
        jnp.bfloat16
    )
    crossed_in = jnp.concatenate([user_part, cand_emb], axis=1)
    low_rank = jnp.dot(crossed_in, cross_down, preferred_element_type=jnp.float32).astype(
        jnp.bfloat16
    )
    up_part = jnp.dot(low_rank, cross_up, preferred_element_type=jnp.float32)
    input_float = crossed_in.astype(jnp.float32)
    crossed = input_float * (up_part + cross_bias) + input_float
    scores = jnp.sum(crossed * score_weight, axis=1)
    return (history_out, scores)


def solution(mesh):
    in_specs = (
        P(("rep", "seq"), None),
        P(("rep", "seq"), None),
        P(),
        P(),
        P("rep"),
        P("rep"),
        P(("rep", "seq"), None),
        P(("rep", "seq")),
        P(),
        P(),
        P(),
        P(),
    )
    out_specs = (P(("rep", "seq"), None), P(("rep", "seq")))
    return jax.shard_map(body, mesh=mesh, in_specs=in_specs, out_specs=out_specs, check_vma=False)
```

time: 97 us -> 83.2 us (0.86)
  Pallas kernels: 92.1 us -> 78.2 us
    pallas_call x1, Pallas kernels: 92.1 us -> 78.2 us  [history_layer(): pl.pallas_call(functools.partial(history_kernel, n, row_tile), out_shape=...]
where the time goes in v1:
time: 83.2 us; the launch traced here: 83 us
  Pallas kernels  78.2 us (94%)
  matrix products  1.48 us (2%)
  local copies, waits for them, and re-layouts  1.36 us (2%)
  other arithmetic  1.09 us (1%)
    pallas_call x1, Pallas kernels, history_layer(): pl.pallas_call(functools.partial(history_kernel, n, row_tile), out_shape=...  78.2 us

profile of v1, /device:TPU:0, one launch (start us, length us, event | category | flops | bytes accessed | tf_op | source)
XLA Modules:
  0.0 83.0 jit_solution(11069856092562268078)
XLA Ops:
  0.6 0.0 copy-start
  0.6 0.0 copy-start.2
  0.7 0.0 copy-start.7
  0.7 0.0 copy-start.3
  0.7 0.0 copy-start.4
  0.7 0.0 copy-start.5
  0.7 0.0 copy-start.6
  0.7 78.2 %history_layer.1 = (bf16[768,1024]{1,0:T(8,128)(2,1)}, f32[16,1,1024]{2,1,0:T(1,128)}) custom-call(s32[8]{0:T(128)} %spans_ref.1, s32[8]{0:T(128)} %tails_ref.1, f32[1,1024]{1,0:T(1,128)} %bitcast.6, bf16[768,4096]{1,0:T(8,128)(2,1)} %proj_ref.1, bf16[768,1024]{1,0:T(8,128)(2,1)} %hist_ref.1, bf16[1024,1024]{1,0:T(8,128)(2,1)} %weight_ref.1), custom_call_target="tpu_custom_call" | custom-call | tf_op jit(solution)/shard_map/history_layer/pallas_call | solution.py:431
  79.0 0.9 %convert_element_type.16 = bf16[16,1,1024]{2,1,0:T(2,128)(2,1)S(1)} convert(f32[16,1,1024]{2,1,0:T(1,128)} %get-tuple-element.5) | non-fusion elementwise | flops 16384 | bytes 98304 | tf_op jit(solution)/shard_map/convert_element_type | solution.py:496
  79.9 0.0 copy-done.2
  79.9 0.1 select_reduce_fusion.1
  80.0 0.0 copy-done.7
  80.0 0.1 select_reduce_fusion
  80.1 0.3 convolution_convert_fusion
  80.4 0.0 copy-done
  80.4 0.0 copy-done.3
  80.4 0.0 copy-done.4
  80.4 0.0 copy-done.5
  80.4 0.0 copy-done.6
  80.4 0.0 copy-start.1
  80.4 1.2 %fusion.3 = f32[128]{0:T(128)} fusion(bf16[128,2048]{1,0:T(8,128)(2,1)S(1)} %copy-done, bf16[2048,128]{1,0:T(8,128)(2,1)S(1)} %copy-done.3, bf16[128,1024]{1,0:T(8,128)(2,1)S(1)} %copy-done.4, bf16[128,1024]{1,0:T(8,128)(2,1)S(1)} %convolution_convert_fusion, f32[2048]{0:T(1024)S(1)} %copy-done.5, f32[2048]{0:T(1024)S(1)} %copy-done.6), kind=kOutput, calls=%fused_computation.4 | convolution fusion | flops 137641856 | bytes 1589760 | tf_op jit(solution)/shard_map/dot_general | solution.py:511
  81.6 0.2 copy-done.1
  81.8 1.1 %copy.20 = bf16[768,1024]{1,0:T(8,128)(2,1)} copy(bf16[768,1024]{1,0:T(8,128)(2,1)S(1)} %copy-done.1) | data formatting | bytes 3145728
  (1 shorter events, 0.0 us)
Async XLA Ops:
  0.6 79.7 %copy-start = (bf16[128,2048]{1,0:T(8,128)(2,1)S(1)}, bf16[128,2048]{1,0:T(8,128)(2,1)}, u32[]{:S(2)}) copy-start(bf16[128,2048]{1,0:T(8,128)(2,1)} %param.21) | copy-start | bytes 1572868
  0.6 79.2 %copy-start.2 = (s32[8]{0:T(128)S(1)}, s32[8]{0:T(128)}, u32[]{:S(2)}) copy-start(s32[8]{0:T(128)} %spans_ref.1) | copy-start | bytes 100
  0.7 79.3 %copy-start.7 = (s32[128]{0:T(128)S(1)}, s32[128]{0:T(128)}, u32[]{:S(2)}) copy-start(s32[128]{0:T(128)} %param.19) | copy-start | bytes 1540
  0.7 79.7 %copy-start.3 = (bf16[2048,128]{1,0:T(8,128)(2,1)S(1)}, bf16[2048,128]{1,0:T(8,128)(2,1)}, u32[]{:S(2)}) copy-start(bf16[2048,128]{1,0:T(8,128)(2,1)} %param.20) | copy-start | bytes 1572868
  0.7 79.7 %copy-start.4 = (bf16[128,1024]{1,0:T(8,128)(2,1)S(1)}, bf16[128,1024]{1,0:T(8,128)(2,1)}, u32[]{:S(2)}) copy-start(bf16[128,1024]{1,0:T(8,128)(2,1)} %param.18) | copy-start | bytes 786436
  0.7 79.7 %copy-start.5 = (f32[2048]{0:T(1024)S(1)}, f32[2048]{0:T(1024)}, u32[]{:S(2)}) copy-start(f32[2048]{0:T(1024)} %param.23) | copy-start | bytes 24580
  0.7 79.7 %copy-start.6 = (f32[2048]{0:T(1024)S(1)}, f32[2048]{0:T(1024)}, u32[]{:S(2)}) copy-start(f32[2048]{0:T(1024)} %param.22) | copy-start | bytes 24580
  80.4 1.4 %copy-start.1 = (bf16[768,1024]{1,0:T(8,128)(2,1)S(1)}, bf16[768,1024]{1,0:T(8,128)(2,1)}, u32[]{:S(2)}) copy-start(bf16[768,1024]{1,0:T(8,128)(2,1)} %get-tuple-element.8) | copy-start | bytes 4718596

commit v2 on v1

v2 whole, which is shorter than its diff:
```python
import functools

import jax
import jax.numpy as jnp
from jax import lax
from jax.experimental import pallas as pl
from jax.experimental.pallas import tpu as pltpu
from jax.sharding import PartitionSpec as P

HEADS = 8
LAG = 3
MESH = pl.DeviceIdType.MESH
OWN, PAIR = range(2)
TO_PAIR, TO_NEAR, TO_FAR, PART, RELAY, PASS, ROW = range(7)
QUERIES, FILLS, GATES, RESIDUAL, WEIGHTS, ROWS, OUT = range(7)


def history_kernel(
    n, row_tile, spans_ref, tails_ref, gain_ref, proj_ref, hist_ref, weight_ref, out_ref, rows_ref,
    kv, queries, gates, residual, weights, attn, final_row, in1, in2, in3, in4, in5, out1, out2,
    rows_in, out_tile, last_query, asked, answers, answer, answered,
    load_sem, once_sem, send_sem, pair_recv, recv1, recv2, recv3, recv4, recv5,
    ask_send, ask_recv, answer_send, answer_recv,
):
    rep, me = lax.axis_index("rep"), lax.axis_index("seq")
    core = lax.rem(me, 2)
    side = lax.rem(me // 2, 2)
    rows, width = residual.shape
    size = width // HEADS
    half_scale = 0.5 * size ** (-0.5)
    tiles = rows // row_tile
    steps = HEADS * tiles
    partner = me + 1 - 2 * core
    even, odd = core == 0, core == 1
    slot_a, slot_b = odd & (side == 0), odd & (side == 1)

    def dev(shift):
        return lax.rem(me + shift + n, n)

    def columns(part, h):
        return pl.ds(pl.multiple_of(part * width + h * size, size), size)

    def load(h, part, target, sem):
        return pltpu.make_async_copy(proj_ref.at[:, columns(part, h)], target, sem)

    def load_queries(h, tile, target, sem):
        block = proj_ref.at[pl.ds(tile * row_tile, row_tile), columns(1, h)]
        return pltpu.make_async_copy(block, target, sem)

    def loads(h):
        return (
            load(h, 2, kv.at[OWN, h, 0], load_sem.at[h]),
            load(h, 3, kv.at[OWN, h, 1], load_sem.at[h]),
        )

    def query_load(h, tile):
        s = tile * HEADS + h
        return load_queries(h, tile, queries.at[s], once_sem.at[QUERIES])

    late = (
        pltpu.make_async_copy(proj_ref.at[:, pl.ds(0, width)], gates, once_sem.at[GATES]),
        pltpu.make_async_copy(hist_ref, residual, once_sem.at[RESIDUAL]),
        pltpu.make_async_copy(weight_ref, weights, once_sem.at[WEIGHTS]),
    )
    fills = [load_queries(s % HEADS, s // HEADS, out1.at[s], once_sem.at[FILLS]) for s in range(LAG)]
    fill_here = slot_b | (slot_a & (me + 4 >= n))

    @pl.when(fill_here)
    def _():
        for copy in fills:
            copy.start()

    for tile in range(tiles):
        @pl.loop(0, HEADS)
        def _(h):
            query_load(h, tile).start()

    @pl.loop(0, HEADS)
    def _(h):
        for copy in loads(h):
            copy.start()

    for copy in late:
        copy.start()

    asked[...] = jnp.zeros_like(asked)
    answered[...] = jnp.zeros_like(answered)

    barrier = pltpu.get_barrier_semaphore()

    @pl.loop(1, n)
    def _(shift):
        pl.semaphore_signal(
            barrier, inc=1, device_id=(rep, dev(shift)), device_id_type=MESH
        )

    seen = (me, me + 1, me + 2, me + 3, me + 4, 4 * (me // 4) + 5)

    def scan_user(user, found):
        start, last, tail, firsts = found
        end = start + spans_ref[user]
        mine = (start <= me) & (me < end)
        return (
            end,
            jnp.where(mine, end - 1, last),
            jnp.where(mine, tails_ref[user], tail),
            tuple(
                jnp.where((start <= s) & (s < end), start, first) for s, first in zip(seen, firsts)
            ),
        )

    zero = jnp.int32(0)
    _, last, tail, firsts = lax.fori_loop(
        0, spans_ref.shape[0], scan_user, (zero, zero, zero, (jnp.int32(2 * n),) * len(seen))
    )
    valid = jnp.where(me == last, tail, rows)
    first_me, first_near, first_far, first_slot = firsts[0], firsts[2], firsts[4], firsts[5]
    final = jnp.clip(valid - 1, 0, rows - 1)
    swapped = first_slot <= 4 * (me // 4) + 3

    pl.semaphore_wait(barrier, n - 1)

    def remote(source, target, send_sem, recv_sem, device):
        return pltpu.make_async_remote_copy(
            src_ref=source,
            dst_ref=target,
            send_sem=send_sem,
            recv_sem=recv_sem,
            device_id=(rep, device),
            device_id_type=MESH,
        )

    def all_here(block, sem):
        pltpu.make_async_copy(block, block, sem).wait()

    def pair(h):
        return remote(kv.at[OWN, h], kv.at[PAIR, h], send_sem.at[TO_PAIR], pair_recv.at[h], partner)

    def near(s):
        return remote(queries.at[s], in1.at[s], send_sem.at[TO_NEAR], recv1.at[s], dev(-2))

    def far(s):
        return remote(queries.at[s], in2.at[s], send_sem.at[TO_FAR], recv2.at[s], dev(-4))

    def across(s):
        return remote(queries.at[s], in5.at[s], send_sem.at[TO_NEAR], recv5.at[s], dev(2))

    def onward(s):
        return remote(in5.at[s], in1.at[s], send_sem.at[PASS], recv1.at[s], dev(-4))

    def far_first(s):
        return remote(queries.at[s], out1.at[s], send_sem.at[TO_FAR], recv2.at[s], dev(-4))

    def near_sum(s):
        return remote(out1.at[s], in3.at[s], send_sem.at[PART], recv3.at[s // HEADS], dev(2))

    def far_sum(s):
        return remote(out2.at[s], in4.at[s], send_sem.at[RELAY], recv4.at[s // HEADS], dev(4))

    def slot(t):
        other = me + 2 - 4 * side
        return remote(out1.at[t], in1.at[t], send_sem.at[PART], recv1.at[t], other)

    def relay(t):
        return remote(in1.at[t], in3.at[t], send_sem.at[RELAY], recv3.at[jnp.maximum(t - LAG, 0) // HEADS], dev(4))

    def ask(back):
        return remote(last_query, asked.at[back], ask_send.at[back], ask_recv.at[back], dev(-back))

    def reply(ahead):
        return remote(answer.at[ahead], answered.at[ahead], answer_send.at[ahead], answer_recv.at[ahead], dev(ahead))

    def row_to(shift):
        return remote(final_row, rows_in.at[me], send_sem.at[ROW], once_sem.at[ROWS], dev(shift))

    def at_last(low, count):
        hit = low + lax.broadcasted_iota(jnp.int32, (16, count), 1) == final
        return jnp.where(hit, 1.0, 0.0).astype(jnp.bfloat16)

    all_here(queries, once_sem.at[QUERIES])

    def send_queries(begin, end):
        @pl.loop(begin, end)
        def _(s):
            @pl.when(even & (side == 1))
            def _():
                near(s).start()

            @pl.when(even & (side == 0) & (me >= 4))
            def _():
                across(s).start()
                far(s).start()

            @pl.when(slot_a & (me >= 4))
            def _():
                @pl.when(s < LAG)
                def _():
                    far_first(s).start()

                @pl.when(s >= LAG)
                def _():
                    far(s).start()

    send_queries(0, 2)

    @pl.loop(0, HEADS)
    def _(h):
        row = sum(
            jnp.dot(
                at_last(tile * row_tile, row_tile), queries[tile * HEADS + h],
                preferred_element_type=jnp.float32,
            )
            for tile in range(tiles)
        )
        last_query[:, pl.ds(pl.multiple_of(h * size, size), size)] = row[0:1]

    asked[0] = last_query[...]

    @pl.loop(0, HEADS)
    def _(h):
        all_here(kv.at[OWN, h], load_sem.at[h])
        pair(h).start()

    for back in (1, 2, 3):
        pl.when(me >= back)(ask(back).start)

    send_queries(2, steps)

    def weigh(q, k):
        half = half_scale * lax.dot_general(
            q, k, (((1,), (1,)), ((), ())), preferred_element_type=jnp.float32
        )
        return half + half * jnp.tanh(half)

    causal = lax.broadcasted_iota(jnp.int32, (row_tile, row_tile), 1) <= (
        lax.broadcasted_iota(jnp.int32, (row_tile, row_tile), 0)
    )

    def head_columns(h):
        return pl.ds(pl.multiple_of(h * size, size), size)

    def over(q, which, h, wanted):
        w = weigh(q, kv[which, h, 0]).astype(jnp.bfloat16)
        part = jnp.dot(w, kv[which, h, 1], preferred_element_type=jnp.float32)
        return jnp.where(wanted, part, 0.0)

    def ask_phase(at):
        @pl.when(at == 2)
        def _():
            for ahead in (1, 2, 3):
                pl.when(me + ahead < n)(ask(ahead).wait_recv)
            visible = (lax.broadcasted_iota(jnp.int32, (8, rows), 0) > 0) | (
                lax.broadcasted_iota(jnp.int32, (8, rows), 1) <= final
            )

            @pl.loop(0, HEADS)
            def _(h):
                q = asked[:, 0, head_columns(h)].astype(jnp.bfloat16)
                w = jnp.where(visible, weigh(q, kv[OWN, h, 0]), 0.0).astype(jnp.bfloat16)
                answers[:, head_columns(h)] = jnp.dot(
                    w, kv[OWN, h, 1], preferred_element_type=jnp.float32
                )

            for ahead in (1, 2, 3):
                answer[ahead] = jnp.where(firsts[ahead] <= me, answers[ahead:ahead + 1], 0.0)

        @pl.when(at == 3)
        def _():
            for ahead in (1, 2, 3):
                pl.when(me + ahead < n)(reply(ahead).start)

    gain = gain_ref[...]

    def finish(x, gate, rest):
        centered = x - jnp.mean(x, axis=1, keepdims=True)
        var = jnp.mean(centered * centered, axis=1, keepdims=True)
        normed = centered * lax.rsqrt(var + 1e-06) * gain
        gated = (normed * gate.astype(jnp.float32)).astype(jnp.bfloat16)
        out = jnp.dot(gated, weights[...], preferred_element_type=jnp.float32)
        return (out + rest.astype(jnp.float32)).astype(jnp.bfloat16)

    def row_phase(at):
        @pl.when(at == 0)
        def _():
            for copy in late:
                copy.wait()
            for back in (1, 2, 3):
                pl.when(me >= back)(reply(back).wait_recv)
            total = answers[0:1] + answered[1] + answered[2] + answered[3]
            pick = at_last(0, rows)
            row = finish(
                jnp.broadcast_to(total, (16, width)),
                jnp.dot(pick, gates[...], preferred_element_type=jnp.float32),
                jnp.dot(pick, residual[...], preferred_element_type=jnp.float32),
            ).astype(jnp.float32)[0:1]
            final_row[...] = row
            rows_in[me] = row

        @pl.when(at == 1)
        def _():
            @pl.loop(1, n)
            def _(shift):
                row_to(shift).start()

    def own(h, tile):
        low, high = tile * row_tile, (tile + 1) * row_tile
        q = queries[tile * HEADS + h]
        edge = jnp.where(causal, weigh(q, kv[OWN, h, 0, low:high]), 0.0).astype(jnp.bfloat16)
        total = jnp.dot(edge, kv[OWN, h, 1, low:high], preferred_element_type=jnp.float32)
        if tile:
            full = weigh(q, kv[OWN, h, 0, :low]).astype(jnp.bfloat16)
            total += jnp.dot(full, kv[OWN, h, 1, :low], preferred_element_type=jnp.float32)
        return total

    def add(h, tile, part):
        low, high = tile * row_tile, (tile + 1) * row_tile
        attn[low:high, head_columns(h)] += part.astype(jnp.float32)

    @pl.when(even)
    def _():
        for tile in range(tiles):
            @pl.loop(0, HEADS)
            def _(h):
                s = tile * HEADS + h
                if tile == 0:
                    ask_phase(h)
                if tile == tiles - 1:
                    row_phase(h - HEADS + 2)

                @pl.when((side == 1) & (me >= 4))
                def _():
                    across(s).wait_recv()
                    onward(s).start()
                    far(s).start()

                attn[tile * row_tile:(tile + 1) * row_tile, head_columns(h)] = own(h, tile)

                @pl.when((s >= 1) & (me + 2 < n))
                def _():
                    near_sum(s - 1).start()

                @pl.when((s >= 1) & (me + 4 < n))
                def _():
                    far_sum(s - 1).start()

                if tile == 0:
                    pair(h).wait_recv()

                @pl.when(me + 2 < n)
                def _():
                    near(s).wait_recv()
                    q = in1[s]
                    total = over(q, OWN, h, first_near <= me)
                    total += over(q, PAIR, h, first_near <= me + 1)
                    out1[s] = total.astype(jnp.bfloat16)

                @pl.when(me + 4 < n)
                def _():
                    far(s).wait_recv()
                    out2[s] = over(in2[s], PAIR, h, first_far <= me + 1).astype(jnp.bfloat16)

        @pl.when(me + 2 < n)
        def _():
            near_sum(steps - 1).start()

        @pl.when(me + 4 < n)
        def _():
            far_sum(steps - 1).start()

    @pl.when(odd)
    def _():
        @pl.when(fill_here)
        def _():
            all_here(out1.at[pl.ds(0, LAG)], once_sem.at[FILLS])

        @pl.when(slot_a & (me + 4 < n))
        def _():
            for s in range(LAG):
                far_first(s).wait_recv()

        for t in range(LAG):
            slot(t).start()

        def pass_on(t):
            slot(t).wait_recv()

            @pl.when((side == 0) & (me + 4 < n))
            def _():
                relay(t).start()

        for tile in range(tiles):
            @pl.loop(0, HEADS)
            def _(h):
                t = tile * HEADS + h
                if tile == 0:
                    pair(h).wait_recv()
                    ask_phase(h)
                if tile == tiles - 1:
                    row_phase(h - HEADS // 2)
                attn[tile * row_tile:(tile + 1) * row_tile, head_columns(h)] = own(h, tile) + over(
                    queries[t], PAIR, h, first_me <= me - 1
                )

                @pl.when(t >= 1)
                def _():
                    slot(t + LAG - 1).start()

                pass_on(t)
                q = in1[t]
                total = over(q, OWN, h, first_near <= me)
                total += over(q, PAIR, h, first_near <= me - 1)
                out1[t + LAG] = total.astype(jnp.bfloat16)

                @pl.when((t + LAG < steps) & (side == 1))
                def _():
                    out1[t + LAG] = jnp.where(swapped, out1[t + LAG], queries[t + LAG])

                @pl.when((t + LAG < steps) & (side == 0) & (me + 4 < n))
                def _():
                    far(t + LAG).wait_recv()
                    out1[t + LAG] = jnp.where(swapped, in2[t + LAG], out1[t + LAG])

        slot(steps + LAG - 1).start()

        @pl.loop(steps, steps + LAG)
        def _(t):
            pass_on(t)

    mine = first_me <= me - 2

    def gather(tile):
        @pl.when(even & (me >= 4))
        def _():
            all_here(in4.at[pl.ds(tile * HEADS, HEADS)], recv4.at[tile])

            @pl.loop(0, HEADS)
            def _(h):
                add(h, tile, in4[tile * HEADS + h])

        @pl.when(even & (me >= 2))
        def _():
            all_here(in3.at[pl.ds(tile * HEADS, HEADS)], recv3.at[tile])

            @pl.loop(0, HEADS)
            def _(h):
                add(h, tile, in3[tile * HEADS + h])

        @pl.when(slot_b)
        def _():
            @pl.loop(0, HEADS)
            def _(h):
                add(h, tile, jnp.where(mine, in1[tile * HEADS + h + LAG], 0.0))

        @pl.when(slot_a & (me >= 4))
        def _():
            if tile == 0:
                all_here(in3.at[pl.ds(0, HEADS + LAG)], recv3.at[0])
            else:
                all_here(in3.at[pl.ds(tile * HEADS + LAG, HEADS)], recv3.at[tile])

            @pl.loop(0, HEADS)
            def _(h):
                add(h, tile, jnp.where(mine, in3[tile * HEADS + h + LAG], 0.0))

    def write(low, high, sem):
        return pltpu.make_async_copy(out_tile.at[pl.ds(low, high - low)], out_ref.at[pl.ds(low, high - low)], sem)

    parts = [(tile * row_tile, (tile + 1) * row_tile) for tile in range(tiles - 1)]
    cut = (tiles - 1) * row_tile + row_tile // 2 // 16 * 16
    parts += [(low, high) for low, high in (((tiles - 1) * row_tile, cut), (cut, rows)) if low < high]

    def close(part):
        low, high = parts[part]
        ids = low + lax.broadcasted_iota(jnp.int32, (high - low, 1), 0)
        x = jnp.where(ids < valid, attn[low:high], 0.0)
        out_tile[low:high] = finish(x, gates[low:high], residual[low:high])
        write(low, high, once_sem.at[OUT]).start()

    for tile in range(tiles - 1):
        gather(tile)
        close(tile)
    gather(tiles - 1)

    for part in range(tiles - 1, len(parts)):
        close(part)

    all_here(kv.at[OWN], send_sem.at[TO_PAIR])

    @pl.when(even & ((side == 1) | (me >= 4)))
    def _():
        all_here(queries, send_sem.at[TO_NEAR])

    @pl.when((even | slot_a) & (me >= 4))
    def _():
        all_here(queries, send_sem.at[TO_FAR])

    @pl.when(even & (side == 1) & (me >= 4))
    def _():
        all_here(in5, send_sem.at[PASS])

    @pl.when(even & (me + 2 < n))
    def _():
        all_here(out1.at[pl.ds(0, steps)], send_sem.at[PART])

    @pl.when(even & (me + 4 < n))
    def _():
        all_here(out2, send_sem.at[RELAY])

    @pl.when(odd)
    def _():
        all_here(out1, send_sem.at[PART])

    @pl.when(slot_a & (me + 4 < n))
    def _():
        all_here(in1, send_sem.at[RELAY])

    for back in (1, 2, 3):
        pl.when(me >= back)(ask(back).wait_send)
        pl.when(me + back < n)(reply(back).wait_send)

    all_here(rows_in.at[pl.ds(0, n - 1)], send_sem.at[ROW])
    all_here(rows_in.at[pl.ds(0, n - 1)], once_sem.at[ROWS])
    rows_ref[...] = rows_in[:, 0, :].astype(jnp.bfloat16)

    all_here(out_tile, once_sem.at[OUT])


def history_layer(n, spans, tails, gain, projected, history_in, out_proj):
    rows, width = history_in.shape
    size = width // HEADS
    row_tile = next(t for t in (384, 256, 128, 64, 32, 16, rows) if rows % t == 0)
    steps = HEADS * (rows // row_tile)
    slots = steps + LAG
    smem = pl.BlockSpec(memory_space=pltpu.SMEM)
    anywhere = pl.BlockSpec(memory_space=pl.ANY)
    vmem = pl.BlockSpec(memory_space=pltpu.VMEM)
    blocks = lambda count: pltpu.VMEM((count, row_tile, size), jnp.bfloat16)
    dma = lambda *shape: pltpu.SemaphoreType.DMA(shape)
    return pl.pallas_call(
        functools.partial(history_kernel, n, row_tile),
        out_shape=(
            jax.ShapeDtypeStruct((rows, width), jnp.bfloat16),
            jax.ShapeDtypeStruct((n, width), jnp.bfloat16),
        ),
        in_specs=[smem, smem, vmem, anywhere, anywhere, anywhere],
        out_specs=(anywhere, vmem),
        scratch_shapes=[
            pltpu.VMEM((2, HEADS, 2, rows, size), jnp.bfloat16),
            blocks(steps),
            pltpu.VMEM((rows, width), jnp.bfloat16),
            pltpu.VMEM((rows, width), jnp.bfloat16),
            pltpu.VMEM((width, width), jnp.bfloat16),
            pltpu.VMEM((rows, width), jnp.float32),
            pltpu.VMEM((1, width), jnp.float32),
            blocks(slots),
            blocks(steps),
            blocks(slots),
            blocks(steps),
            blocks(steps),
            blocks(slots),
            blocks(steps),
            pltpu.VMEM((n, 1, width), jnp.float32),
            pltpu.VMEM((rows, width), jnp.bfloat16),
            pltpu.VMEM((1, width), jnp.float32),
            pltpu.VMEM((8, 1, width), jnp.float32),
            pltpu.VMEM((8, width), jnp.float32),
            pltpu.VMEM((4, 1, width), jnp.float32),
            pltpu.VMEM((4, 1, width), jnp.float32),
            dma(HEADS),
            dma(7),
            dma(7),
            dma(HEADS),
            dma(slots),
            dma(steps),
            dma(rows // row_tile),
            dma(rows // row_tile),
            dma(steps),
            dma(4),
            dma(4),
            dma(4),
            dma(4),
        ],
        compiler_params=pltpu.CompilerParams(
            collective_id=0, has_side_effects=True, vmem_limit_bytes=60 * 1024 * 1024
        ),
        name="history_layer",
    )(spans, tails, gain, projected, history_in, out_proj)


def body(
    projected,
    history_in,
    norm_gain,
    out_proj,
    user_spans,
    user_tails,
    cand_emb,
    cand_user,
    cross_down,
    cross_up,
    cross_bias,
    score_weight,
):
    devices = lax.axis_size("seq")
    history_out, user_rows = history_layer(
        devices, user_spans, user_tails, norm_gain[None, :], projected, history_in, out_proj
    )
    device_ids = jnp.arange(devices, dtype=jnp.int32)
    user_count = user_spans.shape[0]
    users = jnp.arange(user_count, dtype=jnp.int32)
    last_dev = jnp.sum(jnp.where(users[None, :] <= users[:, None], user_spans[None, :], 0), axis=1) - 1
    user_match = cand_user[:, None] == jnp.arange(user_count, dtype=jnp.int32)[None, :]
    cand_dev = jnp.sum(jnp.where(user_match, last_dev[None, :], 0), axis=1)
    selector = (cand_dev[:, None] == device_ids[None, :]).astype(jnp.bfloat16)
    user_part = jnp.dot(selector, user_rows, preferred_element_type=jnp.float32).astype(
        jnp.bfloat16
    )
    crossed_in = jnp.concatenate([user_part, cand_emb], axis=1)
    low_rank = jnp.dot(crossed_in, cross_down, preferred_element_type=jnp.float32).astype(
        jnp.bfloat16
    )
    up_part = jnp.dot(low_rank, cross_up, preferred_element_type=jnp.float32)
    input_float = crossed_in.astype(jnp.float32)
    crossed = input_float * (up_part + cross_bias) + input_float
    scores = jnp.sum(crossed * score_weight, axis=1)
    return (history_out, scores)


def solution(mesh):
    in_specs = (
        P(("rep", "seq"), None),
        P(("rep", "seq"), None),
        P(),
        P(),
        P("rep"),
        P("rep"),
        P(("rep", "seq"), None),
        P(("rep", "seq")),
        P(),
        P(),
        P(),
        P(),
    )
    out_specs = (P(("rep", "seq"), None), P(("rep", "seq")))
    return jax.shard_map(body, mesh=mesh, in_specs=in_specs, out_specs=out_specs, check_vma=False)
```

time: 83.2 us -> 74.3 us (0.89)
  the two profiles are of different devices: /device:TPU:0 before, /device:TPU:25 now
where the time goes in v2:
time: 74.3 us; the launch traced here: 74.1 us
  Pallas kernels  69.5 us (94%)
  matrix products  2.22 us (3%)
  local copies, waits for them, and re-layouts  1.37 us (2%)
  between operations  0.77 us (1%)
    pallas_call x1, Pallas kernels, history_layer(): pl.pallas_call(functools.partial(history_kernel, n, row_tile), out_shape=...  69.5 us

profile of v2, /device:TPU:25, one launch (start us, length us, event | category | flops | bytes accessed | tf_op | source)
XLA Modules:
  0.0 74.1 jit_solution(10914837124489643965)
XLA Ops:
  0.6 0.0 copy-start
  0.6 0.0 copy-start.2
  0.7 0.0 copy-start.7
  0.7 0.0 copy-start.3
  0.7 0.0 copy-start.4
  0.7 0.0 copy-start.5
  0.7 0.0 copy-start.6
  0.7 69.5 %history_layer.1 = (bf16[768,1024]{1,0:T(8,128)(2,1)}, bf16[16,1024]{1,0:T(8,128)(2,1)}) custom-call(s32[8]{0:T(128)} %spans_ref.1, s32[8]{0:T(128)} %tails_ref.1, f32[1,1024]{1,0:T(1,128)} %bitcast.4, bf16[768,4096]{1,0:T(8,128)(2,1)} %proj_ref.1, bf16[768,1024]{1,0:T(8,128)(2,1)} %hist_ref.1, bf16[1024,1024]{1,0:T(8,128)(2,1)} %weight_ref.1), custom_call_target="tpu_custom_call" | custom-call | tf_op jit(solution)/shard_map/history_layer/pallas_call | solution.py:539
  70.2 0.0 copy-done.2
  70.2 0.1 select_reduce_fusion.1
  70.4 0.0 copy-done.7
  70.4 0.1 select_reduce_fusion
  70.4 1.0 %convolution_convert_fusion = bf16[128,1024]{1,0:T(8,128)(2,1)S(1)} fusion(bf16[16,1024]{1,0:T(8,128)(2,1)} %get-tuple-element.5, s32[128]{0:T(128)S(1)} %select_reduce_fusion), kind=kOutput, calls=%fused_computation.5 | convolution fusion | flops 4327424 | bytes 295424 | tf_op jit(solution)/shard_map/dot_general | solution.py:615
  71.5 0.0 copy-done
  71.5 0.0 copy-done.3
  71.5 0.0 copy-done.4
  71.5 0.0 copy-done.5
  71.5 0.0 copy-done.6
  71.5 0.0 copy-start.1
  71.5 1.2 %fusion.3 = f32[128]{0:T(128)} fusion(bf16[128,2048]{1,0:T(8,128)(2,1)S(1)} %copy-done, bf16[2048,128]{1,0:T(8,128)(2,1)S(1)} %copy-done.3, bf16[128,1024]{1,0:T(8,128)(2,1)S(1)} %copy-done.4, bf16[128,1024]{1,0:T(8,128)(2,1)S(1)} %convolution_convert_fusion, f32[2048]{0:T(1024)S(1)} %copy-done.5, f32[2048]{0:T(1024)S(1)} %copy-done.6), kind=kOutput, calls=%fused_computation.4 | convolution fusion | flops 137641856 | bytes 1589760 | tf_op jit(solution)/shard_map/dot_general | solution.py:622
  72.7 0.2 copy-done.1
  72.9 1.1 %copy.15 = bf16[768,1024]{1,0:T(8,128)(2,1)} copy(bf16[768,1024]{1,0:T(8,128)(2,1)S(1)} %copy-done.1) | data formatting | bytes 3145728
  (1 shorter events, 0.0 us)
Async XLA Ops:
  0.6 70.8 %copy-start = (bf16[128,2048]{1,0:T(8,128)(2,1)S(1)}, bf16[128,2048]{1,0:T(8,128)(2,1)}, u32[]{:S(2)}) copy-start(bf16[128,2048]{1,0:T(8,128)(2,1)} %param.21) | copy-start | bytes 1572868
  0.6 69.6 %copy-start.2 = (s32[8]{0:T(128)S(1)}, s32[8]{0:T(128)}, u32[]{:S(2)}) copy-start(s32[8]{0:T(128)} %spans_ref.1) | copy-start | bytes 100
  0.7 69.7 %copy-start.7 = (s32[128]{0:T(128)S(1)}, s32[128]{0:T(128)}, u32[]{:S(2)}) copy-start(s32[128]{0:T(128)} %param.19) | copy-start | bytes 1540
  0.7 70.8 %copy-start.3 = (bf16[2048,128]{1,0:T(8,128)(2,1)S(1)}, bf16[2048,128]{1,0:T(8,128)(2,1)}, u32[]{:S(2)}) copy-start(bf16[2048,128]{1,0:T(8,128)(2,1)} %param.20) | copy-start | bytes 1572868
  0.7 70.8 %copy-start.4 = (bf16[128,1024]{1,0:T(8,128)(2,1)S(1)}, bf16[128,1024]{1,0:T(8,128)(2,1)}, u32[]{:S(2)}) copy-start(bf16[128,1024]{1,0:T(8,128)(2,1)} %param.18) | copy-start | bytes 786436
  0.7 70.8 %copy-start.5 = (f32[2048]{0:T(1024)S(1)}, f32[2048]{0:T(1024)}, u32[]{:S(2)}) copy-start(f32[2048]{0:T(1024)} %param.23) | copy-start | bytes 24580
  0.7 70.8 %copy-start.6 = (f32[2048]{0:T(1024)S(1)}, f32[2048]{0:T(1024)}, u32[]{:S(2)}) copy-start(f32[2048]{0:T(1024)} %param.22) | copy-start | bytes 24580
  71.5 1.4 %copy-start.1 = (bf16[768,1024]{1,0:T(8,128)(2,1)S(1)}, bf16[768,1024]{1,0:T(8,128)(2,1)}, u32[]{:S(2)}) copy-start(bf16[768,1024]{1,0:T(8,128)(2,1)} %get-tuple-element.8) | copy-start | bytes 4718596

commit v3 on v2

--- a/solution.py
+++ b/solution.py
@@ -9,16 +9,18 @@
 
 HEADS = 8
 LAG = 3
+OWN_FROM = 3
 MESH = pl.DeviceIdType.MESH
 OWN, PAIR = range(2)
 TO_PAIR, TO_NEAR, TO_FAR, PART, RELAY, PASS, ROW = range(7)
-QUERIES, FILLS, GATES, RESIDUAL, WEIGHTS, ROWS, OUT = range(7)
+QUERIES, FILLS, GATES, RESIDUAL, WEIGHTS, ROWS, OUT, USERS, CAND, DOWN, UP, BIAS, SCORE, SCORES = range(14)
 
 
 def history_kernel(
-    n, row_tile, spans_ref, tails_ref, gain_ref, proj_ref, hist_ref, weight_ref, out_ref, rows_ref,
+    n, row_tile, spans_ref, tails_ref, gain_ref, proj_ref, hist_ref, weight_ref, user_ref, cand_ref, down_ref, up_ref, bias_ref, score_ref,
+    out_ref, scores_ref,
     kv, queries, gates, residual, weights, attn, final_row, in1, in2, in3, in4, in5, out1, out2,
-    rows_in, out_tile, last_query, asked, answers, answer, answered,
+    rows_in, out_tile, cand_user, cand, down, up, bias, score_weight, scores, last_query, asked, answers, answer, answered,
     load_sem, once_sem, send_sem, pair_recv, recv1, recv2, recv3, recv4, recv5,
     ask_send, ask_recv, answer_send, answer_recv,
 ):
@@ -62,6 +64,15 @@
         pltpu.make_async_copy(hist_ref, residual, once_sem.at[RESIDUAL]),
         pltpu.make_async_copy(weight_ref, weights, once_sem.at[WEIGHTS]),
     )
+    side_loads = (
+        pltpu.make_async_copy(user_ref, cand_user, once_sem.at[USERS]),
+        pltpu.make_async_copy(cand_ref, cand, once_sem.at[CAND]),
+        pltpu.make_async_copy(down_ref, down, once_sem.at[DOWN]),
+        pltpu.make_async_copy(up_ref, up, once_sem.at[UP]),
+        pltpu.make_async_copy(bias_ref, bias, once_sem.at[BIAS]),
+        pltpu.make_async_copy(score_ref, score_weight, once_sem.at[SCORE]),
+    )
+    scores_out = pltpu.make_async_copy(scores, scores_ref, once_sem.at[SCORES])
     fills = [load_queries(s % HEADS, s // HEADS, out1.at[s], once_sem.at[FILLS]) for s in range(LAG)]
     fill_here = slot_b | (slot_a & (me + 4 >= n))
 
@@ -80,7 +91,7 @@
         for copy in loads(h):
             copy.start()
 
-    for copy in late:
+    for copy in late + side_loads:
         copy.start()
 
     asked[...] = jnp.zeros_like(asked)
@@ -316,6 +327,97 @@
         low, high = tile * row_tile, (tile + 1) * row_tile
         attn[low:high, head_columns(h)] += part.astype(jnp.float32)
 
+    mine = first_me <= me - 2
+
+    def gather(tile):
+        @pl.when(even & (me >= 4))
+        def _():
+            all_here(in4.at[pl.ds(tile * HEADS, HEADS)], recv4.at[tile])
+
+            @pl.loop(0, HEADS)
+            def _(h):
+                add(h, tile, in4[tile * HEADS + h])
+
+        @pl.when(even & (me >= 2))
+        def _():
+            all_here(in3.at[pl.ds(tile * HEADS, HEADS)], recv3.at[tile])
+
+            @pl.loop(0, HEADS)
+            def _(h):
+                add(h, tile, in3[tile * HEADS + h])
+
+        @pl.when(slot_b)
+        def _():
+            @pl.loop(0, HEADS)
+            def _(h):
+                add(h, tile, jnp.where(mine, in1[tile * HEADS + h + LAG], 0.0))
+
+        @pl.when(slot_a & (me >= 4))
+        def _():
+            if tile == 0:
+                all_here(in3.at[pl.ds(0, HEADS + LAG)], recv3.at[0])
+            else:
+                all_here(in3.at[pl.ds(tile * HEADS + LAG, HEADS)], recv3.at[tile])
+
+            @pl.loop(0, HEADS)
+            def _(h):
+                add(h, tile, jnp.where(mine, in3[tile * HEADS + h + LAG], 0.0))
+
+    def write(low, high, sem):
+        return pltpu.make_async_copy(out_tile.at[pl.ds(low, high - low)], out_ref.at[pl.ds(low, high - low)], sem)
+
+    parts = [(tile * row_tile, (tile + 1) * row_tile) for tile in range(tiles - 1)]
+    cut = (tiles - 1) * row_tile + row_tile // 2 // 16 * 16
+    parts += [(low, high) for low, high in (((tiles - 1) * row_tile, cut), (cut, rows)) if low < high]
+
+    def close(part):
+        low, high = parts[part]
+        ids = low + lax.broadcasted_iota(jnp.int32, (high - low, 1), 0)
+        x = jnp.where(ids < valid, attn[low:high], 0.0)
+        out_tile[low:high] = finish(x, gates[low:high], residual[low:high])
+        write(low, high, once_sem.at[OUT]).start()
+
+    def close_early():
+        for tile in range(tiles - 1):
+            gather(tile)
+            close(tile)
+
+    def score():
+        for copy in side_loads:
+            copy.wait()
+        all_here(rows_in.at[pl.ds(0, n - 1)], once_sem.at[ROWS])
+        count = cand.shape[0]
+        device = lax.broadcasted_iota(jnp.int32, (n, count), 0)
+        users = cand_user[...]
+
+        def pick_user(user, found):
+            start, chosen = found
+            end = start + spans_ref[user]
+            return end, jnp.where((users == user) & (device == end - 1), 1.0, chosen)
+
+        _, chosen = lax.fori_loop(
+            0, spans_ref.shape[0], pick_user, (zero, jnp.zeros((n, count), jnp.float32))
+        )
+        user_part = lax.dot_general(
+            chosen.astype(jnp.bfloat16), rows_in[:, 0, :].astype(jnp.bfloat16),
+            (((0,), (0,)), ((), ())), preferred_element_type=jnp.float32,
+        ).astype(jnp.bfloat16)
+        low_rank = jnp.dot(user_part, down[:width], preferred_element_type=jnp.float32)
+        low_rank += jnp.dot(cand[...], down[width:], preferred_element_type=jnp.float32)
+        low_rank = low_rank.astype(jnp.bfloat16)
+        total = jnp.zeros((count, 1), jnp.float32)
+        for half, source in ((0, user_part), (1, cand[...])):
+            span = slice(half * width, (half + 1) * width)
+            up_part = jnp.dot(low_rank, up[:, span], preferred_element_type=jnp.float32)
+            value = source.astype(jnp.float32)
+            crossed = value * (up_part + bias[:, span]) + value
+            total += jnp.sum(crossed * score_weight[:, span], axis=1, keepdims=True)
+        diagonal = lax.broadcasted_iota(jnp.int32, (count, count), 0) == (
+            lax.broadcasted_iota(jnp.int32, (count, count), 1)
+        )
+        scores[...] = jnp.sum(jnp.where(diagonal, total, 0.0), axis=0, keepdims=True)
+        scores_out.start()
+
     @pl.when(even)
     def _():
         for tile in range(tiles):
@@ -367,6 +469,9 @@
         def _():
             far_sum(steps - 1).start()
 
+        close_early()
+        score()
+
     @pl.when(odd)
     def _():
         @pl.when(fill_here)
@@ -388,97 +493,57 @@
             def _():
                 relay(t).start()
 
-        for tile in range(tiles):
-            @pl.loop(0, HEADS)
-            def _(h):
-                t = tile * HEADS + h
-                if tile == 0:
-                    pair(h).wait_recv()
-                    ask_phase(h)
-                if tile == tiles - 1:
-                    row_phase(h - HEADS // 2)
-                attn[tile * row_tile:(tile + 1) * row_tile, head_columns(h)] = own(h, tile) + over(
-                    queries[t], PAIR, h, first_me <= me - 1
-                )
-
-                @pl.when(t >= 1)
-                def _():
-                    slot(t + LAG - 1).start()
-
-                pass_on(t)
-                q = in1[t]
-                total = over(q, OWN, h, first_near <= me)
-                total += over(q, PAIR, h, first_near <= me - 1)
-                out1[t + LAG] = total.astype(jnp.bfloat16)
-
-                @pl.when((t + LAG < steps) & (side == 1))
-                def _():
-                    out1[t + LAG] = jnp.where(swapped, out1[t + LAG], queries[t + LAG])
-
-                @pl.when((t + LAG < steps) & (side == 0) & (me + 4 < n))
-                def _():
-                    far(t + LAG).wait_recv()
-                    out1[t + LAG] = jnp.where(swapped, in2[t + LAG], out1[t + LAG])
+        begin = min(OWN_FROM, steps - HEADS)
+
+        @pl.loop(0, steps)
+        def _(t):
+            h = lax.rem(t, HEADS)
+
+            @pl.when(t < HEADS)
+            def _():
+                pair(h).wait_recv()
+
+            ask_phase(t)
+            row_phase(t - steps + HEADS - HEADS // 2)
+            pass_on(t)
+
+            @pl.when(t >= 1)
+            def _():
+                slot(t + LAG - 1).start()
+
+            q = in1[t]
+            total = over(q, OWN, h, first_near <= me)
+            total += over(q, PAIR, h, first_near <= me - 1)
+            out1[t + LAG] = total.astype(jnp.bfloat16)
+
+            @pl.when((t + LAG < steps) & (side == 1))
+            def _():
+                out1[t + LAG] = jnp.where(swapped, out1[t + LAG], queries[t + LAG])
+
+            @pl.when((t + LAG < steps) & (side == 0) & (me + 4 < n))
+            def _():
+                far(t + LAG).wait_recv()
+                out1[t + LAG] = jnp.where(swapped, in2[t + LAG], out1[t + LAG])
+
+            @pl.when((t >= begin) & (t < begin + HEADS))
+            def _():
+                mine_h = t - begin
+                for tile in range(tiles):
+                    attn[tile * row_tile:(tile + 1) * row_tile, head_columns(mine_h)] = own(
+                        mine_h, tile
+                    ) + over(queries[tile * HEADS + mine_h], PAIR, mine_h, first_me <= me - 1)
 
         slot(steps + LAG - 1).start()
-
-        @pl.loop(steps, steps + LAG)
+        pass_on(steps)
+        close_early()
+
+        @pl.loop(steps + 1, steps + LAG - 1)
         def _(t):
             pass_on(t)
 
-    mine = first_me <= me - 2
-
-    def gather(tile):
-        @pl.when(even & (me >= 4))
-        def _():
-            all_here(in4.at[pl.ds(tile * HEADS, HEADS)], recv4.at[tile])
-
-            @pl.loop(0, HEADS)
-            def _(h):
-                add(h, tile, in4[tile * HEADS + h])
-
-        @pl.when(even & (me >= 2))
-        def _():
-            all_here(in3.at[pl.ds(tile * HEADS, HEADS)], recv3.at[tile])
-
-            @pl.loop(0, HEADS)
-            def _(h):
-                add(h, tile, in3[tile * HEADS + h])
-
-        @pl.when(slot_b)
-        def _():
-            @pl.loop(0, HEADS)
-            def _(h):
-                add(h, tile, jnp.where(mine, in1[tile * HEADS + h + LAG], 0.0))
-
-        @pl.when(slot_a & (me >= 4))
-        def _():
-            if tile == 0:
-                all_here(in3.at[pl.ds(0, HEADS + LAG)], recv3.at[0])
-            else:
-                all_here(in3.at[pl.ds(tile * HEADS + LAG, HEADS)], recv3.at[tile])
-
-            @pl.loop(0, HEADS)
-            def _(h):
-                add(h, tile, jnp.where(mine, in3[tile * HEADS + h + LAG], 0.0))
-
-    def write(low, high, sem):
-        return pltpu.make_async_copy(out_tile.at[pl.ds(low, high - low)], out_ref.at[pl.ds(low, high - low)], sem)
-
-    parts = [(tile * row_tile, (tile + 1) * row_tile) for tile in range(tiles - 1)]
-    cut = (tiles - 1) * row_tile + row_tile // 2 // 16 * 16
-    parts += [(low, high) for low, high in (((tiles - 1) * row_tile, cut), (cut, rows)) if low < high]
-
-    def close(part):
-        low, high = parts[part]
-        ids = low + lax.broadcasted_iota(jnp.int32, (high - low, 1), 0)
-        x = jnp.where(ids < valid, attn[low:high], 0.0)
-        out_tile[low:high] = finish(x, gates[low:high], residual[low:high])
-        write(low, high, once_sem.at[OUT]).start()
-
-    for tile in range(tiles - 1):
-        gather(tile)
-        close(tile)
+        score()
+        pass_on(steps + LAG - 1)
+
     gather(tiles - 1)
 
     for part in range(tiles - 1, len(parts)):
@@ -519,13 +584,13 @@
         pl.when(me + back < n)(reply(back).wait_send)
 
     all_here(rows_in.at[pl.ds(0, n - 1)], send_sem.at[ROW])
-    all_here(rows_in.at[pl.ds(0, n - 1)], once_sem.at[ROWS])
-    rows_ref[...] = rows_in[:, 0, :].astype(jnp.bfloat16)
-
+    scores_out.wait()
     all_here(out_tile, once_sem.at[OUT])
 
 
-def history_layer(n, spans, tails, gain, projected, history_in, out_proj):
+def history_layer(
+    n, spans, tails, gain, projected, history_in, out_proj, cand_user, cand_emb, cross_down, cross_up, cross_bias, score_weight
+):
     rows, width = history_in.shape
     size = width // HEADS
     row_tile = next(t for t in (384, 256, 128, 64, 32, 16, rows) if rows % t == 0)
@@ -540,10 +605,10 @@
         functools.partial(history_kernel, n, row_tile),
         out_shape=(
             jax.ShapeDtypeStruct((rows, width), jnp.bfloat16),
-            jax.ShapeDtypeStruct((n, width), jnp.bfloat16),
+            jax.ShapeDtypeStruct(cand_user.shape, jnp.float32),
         ),
-        in_specs=[smem, smem, vmem, anywhere, anywhere, anywhere],
-        out_specs=(anywhere, vmem),
+        in_specs=[smem, smem, vmem] + [anywhere] * 9,
+        out_specs=(anywhere, anywhere),
         scratch_shapes=[
             pltpu.VMEM((2, HEADS, 2, rows, size), jnp.bfloat16),
             blocks(steps),
@@ -561,13 +626,20 @@
             blocks(steps),
             pltpu.VMEM((n, 1, width), jnp.float32),
             pltpu.VMEM((rows, width), jnp.bfloat16),
+            pltpu.VMEM(cand_user.shape, jnp.int32),
+            pltpu.VMEM(cand_emb.shape, jnp.bfloat16),
+            pltpu.VMEM(cross_down.shape, jnp.bfloat16),
+            pltpu.VMEM(cross_up.shape, jnp.bfloat16),
+            pltpu.VMEM(cross_bias.shape, jnp.float32),
+            pltpu.VMEM(score_weight.shape, jnp.float32),
+            pltpu.VMEM(cand_user.shape, jnp.float32),
             pltpu.VMEM((1, width), jnp.float32),
             pltpu.VMEM((8, 1, width), jnp.float32),
             pltpu.VMEM((8, width), jnp.float32),
             pltpu.VMEM((4, 1, width), jnp.float32),
             pltpu.VMEM((4, 1, width), jnp.float32),
             dma(HEADS),
-            dma(7),
+            dma(14),
             dma(7),
             dma(HEADS),
             dma(slots),
@@ -584,7 +656,10 @@
             collective_id=0, has_side_effects=True, vmem_limit_bytes=60 * 1024 * 1024
         ),
         name="history_layer",
-    )(spans, tails, gain, projected, history_in, out_proj)
+    )(
+        spans, tails, gain, projected, history_in, out_proj, cand_user, cand_emb, cross_down, cross_up,
+        cross_bias, score_weight,
+    )
 
 
 def body(
@@ -601,29 +676,11 @@
     cross_bias,
     score_weight,
 ):
-    devices = lax.axis_size("seq")
-    history_out, user_rows = history_layer(
-        devices, user_spans, user_tails, norm_gain[None, :], projected, history_in, out_proj
+    history_out, scores = history_layer(
+        lax.axis_size("seq"), user_spans, user_tails, norm_gain[None, :], projected, history_in, out_proj,
+        cand_user[None, :], cand_emb, cross_down, cross_up, cross_bias[None, :], score_weight[None, :],
     )
-    device_ids = jnp.arange(devices, dtype=jnp.int32)
-    user_count = user_spans.shape[0]
-    users = jnp.arange(user_count, dtype=jnp.int32)
-    last_dev = jnp.sum(jnp.where(users[None, :] <= users[:, None], user_spans[None, :], 0), axis=1) - 1
-    user_match = cand_user[:, None] == jnp.arange(user_count, dtype=jnp.int32)[None, :]
-    cand_dev = jnp.sum(jnp.where(user_match, last_dev[None, :], 0), axis=1)
-    selector = (cand_dev[:, None] == device_ids[None, :]).astype(jnp.bfloat16)
-    user_part = jnp.dot(selector, user_rows, preferred_element_type=jnp.float32).astype(
-        jnp.bfloat16
-    )
-    crossed_in = jnp.concatenate([user_part, cand_emb], axis=1)
-    low_rank = jnp.dot(crossed_in, cross_down, preferred_element_type=jnp.float32).astype(
-        jnp.bfloat16
-    )
-    up_part = jnp.dot(low_rank, cross_up, preferred_element_type=jnp.float32)
-    input_float = crossed_in.astype(jnp.float32)
-    crossed = input_float * (up_part + cross_bias) + input_float
-    scores = jnp.sum(crossed * score_weight, axis=1)
-    return (history_out, scores)
+    return (history_out, scores[0])
 
 
 def solution(mesh):

time: 74.3 us -> 72.5 us (0.976)
  matrix products: 2.22 us -> 0 us
  local copies, waits for them, and re-layouts: 1.37 us -> 3.19 us
  Pallas kernels: 69.5 us -> 68.2 us
    dot_general x2 -> x0, matrix products: 2.22 us -> none  [the longest x1 1.2 us: body(): up_part = jnp.dot(low_rank, cross_up, preferred_element_type=jnp.float32)]
    unnamed x17 -> x4, local copies, waits for them, and re-layouts: 1.37 us -> 3.19 us
    pallas_call x1, Pallas kernels: 69.5 us -> 68.2 us  [history_layer(): pl.pallas_call(functools.partial(history_kernel, n, row_tile), out_shape=...]
where the time goes in v3:
time: 72.5 us; the launch traced here: 72.1 us
  Pallas kernels  68.2 us (94%)
  local copies, waits for them, and re-layouts  3.19 us (4%)
    pallas_call x1, Pallas kernels, history_layer(): pl.pallas_call(functools.partial(history_kernel, n, row_tile), out_shape=...  68.2 us
    unnamed x4, local copies, waits for them, and re-layouts  3.19 us

profile of v3, /device:TPU:25, one launch (start us, length us, event | category | flops | bytes accessed | tf_op | source)
XLA Modules:
  0.0 72.1 jit_solution(8257274489558558432)
XLA Ops:
  0.6 68.2 %history_layer.1 = (bf16[768,1024]{1,0:T(8,128)(2,1)}, f32[1,128]{1,0:T(1,128)}) custom-call(s32[8]{0:T(128)} %spans_ref.1, s32[8]{0:T(128)} %tails_ref.1, f32[1,1024]{1,0:T(1,128)} %bitcast.7, bf16[768,4096]{1,0:T(8,128)(2,1)} %proj_ref.1, bf16[768,1024]{1,0:T(8,128)(2,1)} %hist_ref.1, bf16[1024,1024]{1,0:T(8,128)(2,1)} %weight_ref.1, s32[1,128]{1,0:T(1,128)} %bitcast.8, ...), custom_call_target="tpu_custom_call" | custom-call | tf_op jit(solution)/shard_map/history_layer/pallas_call | solution.py:604
  68.9 0.0 copy-start
  68.9 2.7 %copy.16 = bf16[768,1024]{1,0:T(8,128)(2,1)} copy(bf16[768,1024]{1,0:T(8,128)(2,1)} %get-tuple-element.8) | data formatting | bytes 3145728
  71.6 0.0 copy-done
  71.6 0.5 copy.17
Async XLA Ops:
  68.9 2.7 %copy-start = (f32[1,128]{1,0:T(1,128)S(1)}, f32[1,128]{1,0:T(1,128)}, u32[]{:S(2)}) copy-start(f32[1,128]{1,0:T(1,128)} %get-tuple-element.5) | copy-start | bytes 1540

commit v4 on v3

--- a/solution.py
+++ b/solution.py
@@ -9,7 +9,8 @@
 
 HEADS = 8
 LAG = 3
-OWN_FROM = 3
+OWN_FROM = 2
+AHEAD = 2
 MESH = pl.DeviceIdType.MESH
 OWN, PAIR = range(2)
 TO_PAIR, TO_NEAR, TO_FAR, PART, RELAY, PASS, ROW = range(7)
@@ -200,7 +201,6 @@
             @pl.when(even & (side == 0) & (me >= 4))
             def _():
                 across(s).start()
-                far(s).start()
 
             @pl.when(slot_a & (me >= 4))
             def _():
@@ -212,7 +212,7 @@
                 def _():
                     far(s).start()
 
-    send_queries(0, 2)
+    send_queries(0, LAG)
 
     @pl.loop(0, HEADS)
     def _(h):
@@ -235,7 +235,12 @@
     for back in (1, 2, 3):
         pl.when(me >= back)(ask(back).start)
 
-    send_queries(2, steps)
+    send_queries(LAG, steps)
+
+    @pl.when(even & (side == 0) & (me >= 4))
+    def _():
+        for s in range(AHEAD):
+            far(s).start()
 
     def weigh(q, k):
         half = half_scale * lax.dot_general(
@@ -429,6 +434,10 @@
                 if tile == tiles - 1:
                     row_phase(h - HEADS + 2)
 
+                @pl.when((side == 0) & (me >= 4) & (s + AHEAD < steps))
+                def _():
+                    far(s + AHEAD).start()
+
                 @pl.when((side == 1) & (me >= 4))
                 def _():
                     across(s).wait_recv()
@@ -478,12 +487,11 @@
         def _():
             all_here(out1.at[pl.ds(0, LAG)], once_sem.at[FILLS])
 
-        @pl.when(slot_a & (me + 4 < n))
-        def _():
-            for s in range(LAG):
-                far_first(s).wait_recv()
-
         for t in range(LAG):
+            @pl.when(slot_a & (me + 4 < n))
+            def _():
+                far_first(t).wait_recv()
+
             slot(t).start()
 
         def pass_on(t):
@@ -535,14 +543,22 @@
 
         slot(steps + LAG - 1).start()
         pass_on(steps)
+        relays = (side == 0) & (me + 4 < n)
+
+        @pl.when(relays)
+        def _():
+            @pl.loop(steps + 1, steps + LAG)
+            def _(t):
+                pass_on(t)
+
         close_early()
-
-        @pl.loop(steps + 1, steps + LAG - 1)
-        def _(t):
-            pass_on(t)
-
         score()
-        pass_on(steps + LAG - 1)
+
+        @pl.when(~relays)
+        def _():
+            @pl.loop(steps + 1, steps + LAG)
+            def _(t):
+                pass_on(t)
 
     gather(tiles - 1)
 

time: 72.5 us -> 71.8 us (level)
  Pallas kernels: 68.2 us -> 67.4 us
    pallas_call x1, Pallas kernels: 68.2 us -> 67.4 us  [history_layer(): pl.pallas_call(functools.partial(history_kernel, n, row_tile), out_shape=...]
where the time goes in v4:
time: 71.8 us; the launch traced here: 71.2 us
  Pallas kernels  67.4 us (94%)
  local copies, waits for them, and re-layouts  3.19 us (4%)
    pallas_call x1, Pallas kernels, history_layer(): pl.pallas_call(functools.partial(history_kernel, n, row_tile), out_shape=...  67.4 us
    unnamed x4, local copies, waits for them, and re-layouts  3.19 us

profile of v4, /device:TPU:25, one launch (start us, length us, event | category | flops | bytes accessed | tf_op | source)
XLA Modules:
  0.0 71.2 jit_solution(17646024311674179260)
XLA Ops:
  0.6 67.4 %history_layer.1 = (bf16[768,1024]{1,0:T(8,128)(2,1)}, f32[1,128]{1,0:T(1,128)}) custom-call(s32[8]{0:T(128)} %spans_ref.1, s32[8]{0:T(128)} %tails_ref.1, f32[1,1024]{1,0:T(1,128)} %bitcast.7, bf16[768,4096]{1,0:T(8,128)(2,1)} %proj_ref.1, bf16[768,1024]{1,0:T(8,128)(2,1)} %hist_ref.1, bf16[1024,1024]{1,0:T(8,128)(2,1)} %weight_ref.1, s32[1,128]{1,0:T(1,128)} %bitcast.8, ...), custom_call_target="tpu_custom_call" | custom-call | tf_op jit(solution)/shard_map/history_layer/pallas_call | solution.py:620
  68.0 0.0 copy-start
  68.0 2.7 %copy.16 = bf16[768,1024]{1,0:T(8,128)(2,1)} copy(bf16[768,1024]{1,0:T(8,128)(2,1)} %get-tuple-element.8) | data formatting | bytes 3145728
  70.7 0.0 copy-done
  70.7 0.5 copy.17
Async XLA Ops:
  68.0 2.7 %copy-start = (f32[1,128]{1,0:T(1,128)S(1)}, f32[1,128]{1,0:T(1,128)}, u32[]{:S(2)}) copy-start(f32[1,128]{1,0:T(1,128)} %get-tuple-element.5) | copy-start | bytes 1540
